TPU v7x, 32 devices: a whole 2x2x4 slice. The times are simulated.
32 devices in a mesh: tensor: 4 (over z), seq: 8 (over y, x, core).
Axes of the slice: x: 2, y: 2, z: 4, core: 2. Of those that a mesh axis runs over, the one named last changes fastest.
Arguments:
- teacher_q: bfloat16 [4096, 8192], P('seq', 'tensor'), may hold values from -24 to 24
- teacher_v: bfloat16 [4096, 8192], P('seq', 'tensor'), may hold values from -24 to 24
- student_q: bfloat16 [4096, 2048], P('seq'), may hold values from -24 to 24
- student_v: bfloat16 [4096, 2048], P('seq'), may hold values from -24 to 24
Outputs:
- grad_q: bfloat16 [4096, 2048], P('seq')
- grad_v: bfloat16 [4096, 2048], P('seq')
All inputs are finite; a program needn't handle non-finite values.
Results may differ from a plain program's by a relative error of at most 0.0095.
Values may be sent and summed in bfloat16 or wider, within the bound.
A program may use at most 128 MiB of HBM per device.

v0:
```python
import jax
import jax.numpy as jnp
from jax import lax
from jax.sharding import PartitionSpec as P

HEADS = 32
SEQS = 2


def from_partner(array, axis, distance):
    return lax.ppermute(array, axis, [(i, i ^ 1 << distance) for i in range(lax.axis_size(axis))])


def head_terms(teach_query, teach_key, stud_query, stud_key, teach_dim, stud_dim):
    teach_scores = jnp.dot(
        teach_query, teach_key.T, preferred_element_type=jnp.float32
    ) * teach_dim ** (-0.5)
    stud_scores = jnp.dot(
        stud_query, stud_key.T, preferred_element_type=jnp.float32
    ) * stud_dim ** (-0.5)
    teach_prob = jax.nn.softmax(teach_scores, axis=-1)
    stud_prob = jax.nn.softmax(stud_scores, axis=-1)
    coef = (256.0 * stud_dim ** (-0.5) * (stud_prob - teach_prob)).astype(jnp.bfloat16)
    query_grad = jnp.dot(coef, stud_key, preferred_element_type=jnp.float32)
    key_grad = jnp.einsum("qk,qd->kd", coef, stud_query, preferred_element_type=jnp.float32)
    return (query_grad, key_grad)


def relate(teach_own, teach_keys, stud_own, stud_keys, per_dev, teach_dim, stud_dim):
    tok_rows = teach_own.shape[0]
    teach_query = teach_own.reshape(tok_rows, per_dev, teach_dim).transpose(1, 0, 2)
    teach_key = teach_keys.reshape(-1, per_dev, teach_dim).transpose(1, 0, 2)
    stud_query = stud_own.reshape(tok_rows, per_dev, stud_dim).transpose(1, 0, 2)
    stud_key = stud_keys.reshape(-1, per_dev, stud_dim).transpose(1, 0, 2)

    def one_head(group):
        return head_terms(group[0], group[1], group[2], group[3], teach_dim, stud_dim)

    query_grad, key_grad = lax.map(one_head, (teach_query, teach_key, stud_query, stud_key))
    return (
        query_grad.transpose(1, 0, 2).reshape(tok_rows, per_dev * stud_dim),
        key_grad.transpose(1, 0, 2).reshape(-1, per_dev * stud_dim),
    )


def shards(teacher_q, teacher_v, student_q, student_v):
    n_tensor = lax.axis_size("tensor")
    n_seq = lax.axis_size("seq")
    per_dev = HEADS // n_tensor
    group_size = n_seq // SEQS
    level_count = group_size.bit_length() - 1
    seq_index = lax.axis_index("seq")
    member = seq_index % group_size
    teach_dim = teacher_q.shape[1] // per_dev
    stud_dim = student_q.shape[1] // HEADS
    own_width = per_dev * stud_dim
    offset = lax.axis_index("tensor") * own_width
    own_q = lax.dynamic_slice_in_dim(student_q, offset, own_width, 1)
    own_v = lax.dynamic_slice_in_dim(student_v, offset, own_width, 1)
    key_tq, key_tv, key_sq, key_sv = (teacher_q, teacher_v, own_q, own_v)
    for bit_num in range(level_count):
        partner = from_partner((key_tq, key_tv, key_sq, key_sv), "seq", bit_num)
        upper_half = member // 2**bit_num % 2 == 1
        joined = []
        for mine, theirs in zip((key_tq, key_tv, key_sq, key_sv), partner):
            joined.append(
                jnp.where(
                    upper_half,
                    jnp.concatenate([theirs, mine], 0),
                    jnp.concatenate([mine, theirs], 0),
                )
            )
        key_tq, key_tv, key_sq, key_sv = joined
    q_query, q_key = relate(teacher_q, key_tq, own_q, key_sq, per_dev, teach_dim, stud_dim)
    v_query, v_key = relate(teacher_v, key_tv, own_v, key_sv, per_dev, teach_dim, stud_dim)
    returned = jnp.concatenate([q_key, v_key], axis=1)
    for bit_num in reversed(range(level_count)):
        half_rows = returned.shape[0] // 2
        upper_half = member // 2**bit_num % 2 == 1
        low_part = returned[:half_rows]
        high_part = returned[half_rows:]
        kept = jnp.where(upper_half, high_part, low_part)
        outgoing = jnp.where(upper_half, low_part, high_part)
        returned = kept + from_partner(outgoing.astype(jnp.bfloat16), "seq", bit_num).astype(
            outgoing.dtype
        )
    head_q = (q_query + returned[:, :own_width]).astype(jnp.bfloat16)
    head_v = (v_query + returned[:, own_width:]).astype(jnp.bfloat16)
    full_q, full_v = (
        lax.all_gather(head_q, "tensor", axis=1, tiled=True),
        lax.all_gather(head_v, "tensor", axis=1, tiled=True),
    )
    return (full_q, full_v)


def solution(mesh):
    in_specs = (P("seq", "tensor"), P("seq", "tensor"), P("seq", None), P("seq", None))
    out_specs = (P("seq", None), P("seq", None))
    return jax.shard_map(shards, mesh=mesh, in_specs=in_specs, out_specs=out_specs, check_vma=False)
```

profile of v0, /device:TPU:0, one launch (start us, length us, event | category | flops | bytes accessed | tf_op | source)
XLA Modules:
  0.0 555.9 jit_solution(9372963571637865610)
XLA Ops:
  7.2 4.0 copy.11
  11.7 4.1 collective-permute-done.2
  15.9 6.6 %maximum_select_fusion.2 = bf16[1024,2048]{0,1:T(8,128)(2,1)} fusion(bf16[512,2048]{0,1:T(8,128)(2,1)} %copy.11, bf16[512,2048]{0,1:T(8,128)(2,1)} %collective-permute-done.2, pred[]{:T(512)S(6)} %eq.15), kind=kLoop, calls=%fused_computation.66 | loop fusion | flops 18874368 | bytes 8388609 | tf_op jit(solution)/shard_map/jit(_where)/select_n | solution.py:67
  22.5 2.9 collective-permute-start.3
  25.7 3.9 copy.20
  33.3 2.6 maximum_select_fusion.8
  43.0 96.5 %collective-permute-done.1 = bf16[1024,512]{0,1:T(8,128)(2,1)} collective-permute-done((bf16[1024,512]{0,1:T(8,128)(2,1)}, bf16[1024,512]{0,1:T(8,128)(2,1)}, u32[]{:S(2)}, u32[]{:S(2)}) %collective-permute-start.1) | collective-permute-done | bytes 1048608 | tf_op jit(solution)/shard_map/ppermute | solution.py:11
  139.5 3.7 fusion.47
  143.2 18.3 %collective-permute-done.5 = bf16[1024,512]{0,1:T(8,128)(2,1)} collective-permute-done((bf16[1024,512]{0,1:T(8,128)(2,1)}, bf16[1024,512]{0,1:T(8,128)(2,1)}, u32[]{:S(2)}, u32[]{:S(2)}) %collective-permute-start.5) | collective-permute-done | bytes 1048608 | tf_op jit(solution)/shard_map/ppermute | solution.py:11
  161.5 3.7 fusion.48
  165.1 4.9 maximum_select_fusion.4
  171.8 5.3 maximum_select_fusion.3
  177.1 5.0 maximum_select_fusion.5
  182.1 8.9 %fusion.44 = bf16[8,2048,256]{1,2,0:T(8,128)(2,1)} fusion(bf16[1024,8,256]{0,2,1:T(8,128)(2,1)S(1)} %maximum_select_fusion.3, bf16[1024,8,256]{0,2,1:T(8,128)(2,1)} %bitcast.19, pred[]{:T(512)S(6)} %eq.14), kind=kLoop, calls=%fused_computation.59 | loop fusion | flops 37748736 | bytes 16777216 | tf_op jit(solution)/shard_map/transpose | solution.py:32
  191.0 2.5 broadcast.48.clone.1
  194.7 90.5 %while.24 = (s32[]{:T(128)}, f32[8,512,64]{1,2,0:T(8,128)}, f32[8,2048,64]{1,2,0:T(8,128)}, bf16[8,512,64]{1,2,0:T(8,128)(2,1)S(1)}, bf16[8,2048,64]{1,2,0:T(8,1...) while((s32[]{:T(128)}, f32[8,512,64]{1,2,0:T(8,128)}, ...), condition=%wide.region_5.6_spmd, body=%wide.region_0.5_spmd.sunk | while | flops 959444992 | bytes 34103380 | solution.py:39
  196.4 2.1 multiply_reduce_fusion.9
  203.6 2.4 fusion.74
  214.9 2.4 fusion.74
  226.3 2.4 fusion.74
  237.6 2.4 fusion.74
  241.7 2.1 multiply_reduce_fusion.9
  248.9 2.4 fusion.74
  260.2 2.4 fusion.74
  271.5 2.4 fusion.74
  282.8 2.4 fusion.74
  285.2 11.2 %fusion.45 = bf16[8,2048,256]{1,2,0:T(8,128)(2,1)} fusion(bf16[1024,8,256]{0,2,1:T(8,128)(2,1)} %maximum_select_fusion.5, bf16[1024,8,256]{0,2,1:T(8,128)(2,1)} %bitcast.33, pred[]{:T(512)S(6)} %eq.14), kind=kLoop, calls=%fused_computation.61 | loop fusion | flops 37748736 | bytes 16777216 | tf_op jit(solution)/shard_map/transpose | solution.py:32
  296.4 2.5 broadcast.48.clone
  300.0 90.5 %while.25 = (s32[]{:T(128)}, f32[8,512,64]{1,2,0:T(8,128)}, f32[8,2048,64]{1,2,0:T(8,128)}, bf16[8,512,64]{1,2,0:T(8,128)(2,1)S(1)}, bf16[8,2048,64]{1,2,0:T(8,1...) while((s32[]{:T(128)}, f32[8,512,64]{1,2,0:T(8,128)}, ...), condition=%wide.region_11.12_spmd, body=%wide.region_6.11_spmd.sunk | while | flops 959444992 | bytes 34103380 | solution.py:39
  309.0 2.4 fusion.81
  313.1 2.1 multiply_reduce_fusion.11
  320.3 2.4 fusion.81
  331.6 2.4 fusion.81
  342.9 2.4 fusion.81
  354.2 2.4 fusion.81
  365.5 2.4 fusion.81
  376.8 2.4 fusion.81
  381.0 2.1 multiply_reduce_fusion.11
  388.1 2.4 fusion.81
  390.5 4.1 select_convert_fusion
  394.9 46.3 %collective-permute-done.8 = bf16[1024,1024]{0,1:T(8,128)(2,1)S(1)} collective-permute-done((bf16[1024,1024]{0,1:T(8,128)(2,1)S(1)}, bf16[1024,1024]{0,1:T(8,128)(2,1)S(1)}, u32[]{:S(2)}, u32[]{:S(2)}) %collective-permute-start.8) | collective-permute-done | bytes 2097184 | tf_op jit(solution)/shard_map/ppermute | solution.py:11
  441.2 4.2 convert_add_fusion
  445.7 2.6 collective-permute-done.9
  449.0 2.9 fusion.49
  452.7 45.6 %all-gather.3.cloned.1.call-done = bf16[512,2048]{0,1:T(8,128)(2,1)} async-done(((bf16[512,512]{0,1:T(8,128)(2,1)}), bf16[512,2048]{0,1:T(8,128)(2,1)}) %all-gather.3.cloned.1.call-update) | async-done | bytes 2097168 | tf_op jit(solution)/shard_map/all_gather | solution.py:90
  498.3 3.9 copy.28
  502.2 42.9 %all-gather.5.cloned.1.call-done = bf16[512,2048]{0,1:T(8,128)(2,1)} async-done(((bf16[512,512]{0,1:T(8,128)(2,1)}), bf16[512,2048]{0,1:T(8,128)(2,1)}) %all-gather.5.cloned.1.call-update) | async-done | bytes 2097168 | tf_op jit(solution)/shard_map/all_gather | solution.py:91
  545.1 3.9 copy.29
  (111 shorter events, 152.1 us)
Async XLA Ops:
  7.2 18.2 %copy-start = (bf16[512,2048]{1,0:T(8,128)(2,1)S(1)}, bf16[512,2048]{1,0:T(8,128)(2,1)}, u32[]{:S(2)}) copy-start(bf16[512,2048]{1,0:T(8,128)(2,1)} %param.10) | copy-start | bytes 6291460
  7.2 491.1 %all-gather.3.cloned.1.call-start = ((), (), s32[]{:S(2)}) async-start(), calls=%async_computation | async-start | bytes 2621440 | tf_op jit(solution)/shard_map/all_gather | solution.py:90
  11.3 4.6 collective-permute-start.2
  22.5 159.6 %collective-permute-start.3 = (bf16[1024,2048]{0,1:T(8,128)(2,1)}, bf16[1024,2048]{0,1:T(8,128)(2,1)}, u32[]{:S(2)}, u32[]{:S(2)}) collective-permute-start(bf16[1024,2048]{0,1:T(8,128)(2,1)} %maximum_select_fusion.2), channel_id=1, source_target_pairs={{0,2},{1,3},{2,0},{3,1},{4,6},{5,7},{6,4},{7,5},{8,10},{9,11},{10,... | collective-permute-start | bytes 12582920 | tf_op jit(solution)/shard_map/ppermute | solution.py:11
  25.6 7.7 %collective-permute-start = (bf16[512,512]{0,1:T(8,128)(2,1)S(1)}, bf16[512,512]{0,1:T(8,128)(2,1)}, u32[]{:S(2)}, u32[]{:S(2)}) collective-permute-start(bf16[512,512]{0,1:T(8,128)(2,1)S(1)} %copy.38), channel_id=1, source_target_pairs={{0,1},{1,0},{2,3},{3,2},{4,5},{5,4},{6,7},{7,6},{8,9},{9,8},{10,11... | collective-permute-start | bytes 1572872 | tf_op jit(solution)/shard_map/ppermute | solution.py:11
  29.6 135.5 %collective-permute-start.6 = (bf16[512,2048]{0,1:T(8,128)(2,1)}, bf16[512,2048]{0,1:T(8,128)(2,1)S(1)}, u32[]{:S(2)}, u32[]{:S(2)}) collective-permute-start(bf16[512,2048]{0,1:T(8,128)(2,1)} %copy.20), channel_id=1, source_target_pairs={{0,1},{1,0},{2,3},{3,2},{4,5},{5,4},{6,7},{7,6},{8,9},{9,8},{10,11... | collective-permute-start | bytes 6291464 | tf_op jit(solution)/shard_map/ppermute | solution.py:11
  33.2 2.8 collective-permute-start.4
  35.9 103.6 %collective-permute-start.1 = (bf16[1024,512]{0,1:T(8,128)(2,1)}, bf16[1024,512]{0,1:T(8,128)(2,1)}, u32[]{:S(2)}, u32[]{:S(2)}) collective-permute-start(bf16[1024,512]{0,1:T(8,128)(2,1)} %maximum_select_fusion.8), channel_id=1, source_target_pairs={{0,2},{1,3},{2,0},{3,1},{4,6},{5,7},{6,4},{7,5},{8,10},{9,11},{10,... | collective-permute-start | bytes 3145736 | tf_op jit(solution)/shard_map/ppermute | solution.py:11
  36.0 0.8 copy-start.2
  38.1 123.4 %collective-permute-start.5 = (bf16[1024,512]{0,1:T(8,128)(2,1)}, bf16[1024,512]{0,1:T(8,128)(2,1)}, u32[]{:S(2)}, u32[]{:S(2)}) collective-permute-start(bf16[1024,512]{0,1:T(8,128)(2,1)} %maximum_select_fusion.10), channel_id=1, source_target_pairs={{0,2},{1,3},{2,0},{3,1},{4,6},{5,7},{6,4},{7,5},{8,10},{9,11},{10,... | collective-permute-start | bytes 3145736 | tf_op jit(solution)/shard_map/ppermute | solution.py:11
  170.1 115.1 %collective-permute-start.7 = (bf16[1024,2048]{0,1:T(8,128)(2,1)}, bf16[1024,2048]{0,1:T(8,128)(2,1)}, u32[]{:S(2)}, u32[]{:S(2)}) collective-permute-start(bf16[1024,2048]{0,1:T(8,128)(2,1)} %maximum_select_fusion.4), channel_id=1, source_target_pairs={{0,2},{1,3},{2,0},{3,1},{4,6},{5,7},{6,4},{7,5},{8,10},{9,11},{10,... | collective-permute-start | bytes 12582920 | tf_op jit(solution)/shard_map/ppermute | solution.py:11
  394.6 46.6 %collective-permute-start.8 = (bf16[1024,1024]{0,1:T(8,128)(2,1)S(1)}, bf16[1024,1024]{0,1:T(8,128)(2,1)S(1)}, u32[]{:S(2)}, u32[]{:S(2)}) collective-permute-start(bf16[1024,1024]{0,1:T(8,128)(2,1)S(1)} %select_convert_fusion), channel_id=1, source_target_pairs={{0,2},{1,3},{2,0},{3,1},{4,6},{5,7},{6,4},{7,5},{8,10},{9,11},{10,... | collective-permute-start | bytes 6291464 | tf_op jit(solution)/shard_map/ppermute | solution.py:11
  445.6 2.7 collective-permute-start.9
  451.9 93.2 %all-gather.5.cloned.1.call-start = ((), (), s32[]{:S(2)}) async-start(), calls=%async_computation.1 | async-start | bytes 2621440 | tf_op jit(solution)/shard_map/all_gather | solution.py:91
  452.7 96.4 %copy-start.1 = (bf16[512,2048]{1,0:T(8,128)(2,1)S(1)}, bf16[512,2048]{1,0:T(8,128)(2,1)}, u32[]{:S(2)}) copy-start(bf16[512,2048]{1,0:T(8,128)(2,1)} %param.10) | copy-start | bytes 6291460
Sparse Core Ops, SparseCore 0:
  452.0 46.2 all-gather.2
  500.5 44.6 all-gather.4
where the time goes:
time: 558 us; the launch traced here: 556 us
  waiting for transfers between devices  257 us (46%)
  other arithmetic  128 us (23%)
  matrix products  121 us (22%)
  local copies, waits for them, and re-layouts  27.2 us (5%)
  between operations  14.2 us (3%)
  starting transfers between devices  8.22 us (1%)
    ppermute x10, waiting for transfers between devices, from_partner(): lax.ppermute(array, axis, [(i, i ^ 1 << distance) for i in range(lax.axis...  168 us
    all_gather x1, waiting for transfers between devices, shards(): lax.all_gather(head_q, 'tensor', axis=1, tiled=True)  45.6 us
    all_gather x1, waiting for transfers between devices, shards(): lax.all_gather(head_v, 'tensor', axis=1, tiled=True)  42.9 us
    dot_general x16, matrix products, head_terms(): query_grad = jnp.dot(coef, stud_key, preferred_element_type=jnp.float32)  37.8 us
    dot_general x16, matrix products, head_terms(): jnp.dot(teach_query, teach_key.T, preferred_element_type=jnp.float32)  34.1 us
    convert_element_type x16, other arithmetic, head_terms(): (256.0 * stud_dim ** (-0.5) * (stud_prob - teach_prob)).astype(jnp.bfloat16)  31.4 us
    select_n x8, other arithmetic, shards(): jnp.where(upper_half, jnp.concatenate([theirs, mine], 0), jnp.concatenate...  28.7 us
    reduce_sum x16, other arithmetic, head_terms(): stud_prob = jax.nn.softmax(stud_scores, axis=-1)  28.5 us
  transfers between devices with their start and end apart: 12, of which 7 were waited for; matrix products, arithmetic and copies ran while one was open for 26% of the time, Pallas kernels for 0%

commit v1 on v0

--- a/solution.py
+++ b/solution.py
@@ -5,6 +5,27 @@
 
 HEADS = 32
 SEQS = 2
+
+
+def collect(x, axis, dim):
+    length, index, rows = (lax.axis_size(axis), lax.axis_index(axis), x.shape[dim])
+    ahead = [(i, (i + 1) % length) for i in range(length)]
+    downward = [(i, (i - 1) % length) for i in range(length)]
+    out = jnp.zeros((*x.shape[:dim], length * rows, *x.shape[dim + 1 :]), x.dtype)
+    out = lax.dynamic_update_slice_in_dim(out, x, index * rows, axis=dim)
+    from_left = from_right = x
+    half = length // 2
+    for hop in range(1, half + 1):
+        from_left = lax.ppermute(from_left, axis, ahead)
+        out = lax.dynamic_update_slice_in_dim(
+            out, from_left, (index - hop) % length * rows, axis=dim
+        )
+        if hop < length - half:
+            from_right = lax.ppermute(from_right, axis, downward)
+            out = lax.dynamic_update_slice_in_dim(
+                out, from_right, (index + hop) % length * rows, axis=dim
+            )
+    return out
 
 
 def from_partner(array, axis, distance):
@@ -88,7 +109,7 @@
     head_v = (v_query + returned[:, own_width:]).astype(jnp.bfloat16)
     full_q, full_v = (
         lax.all_gather(head_q, "tensor", axis=1, tiled=True),
-        lax.all_gather(head_v, "tensor", axis=1, tiled=True),
+        collect(head_v, "tensor", 1),
     )
     return (full_q, full_v)
 

time: 558 us -> 537 us (0.962)
  waiting for transfers between devices: 257 us -> 216 us
  starting transfers between devices: 8.22 us -> 23.2 us
    all_gather x1 -> x0, waiting for transfers between devices: 42.9 us -> none  [shards(): lax.all_gather(head_v, 'tensor', axis=1, tiled=True)]
    ppermute x0 -> x3, waiting for transfers between devices: none -> 42.8 us  [the longest x2 23.2 us: collect(): from_left = lax.ppermute(from_left, axis, ahead)]
    all_gather x1, waiting for transfers between devices: 45.6 us -> 5.57 us  [shards(): lax.all_gather(head_q, 'tensor', axis=1, tiled=True)]
    ppermute x0 -> x3, starting transfers between devices: none -> 15 us  [the longest x2 12.7 us: collect(): from_left = lax.ppermute(from_left, axis, ahead)]
    unnamed x12 -> x11, local copies, waits for them, and re-layouts: 18.1 us -> 14.1 us
  transfers between devices with their start and end apart: 12 -> 14, of which waited for: 7 -> 9; matrix products, arithmetic and copies ran while one was open for 26% -> 28% of each run, Pallas kernels for 0% -> 0%
where the time goes in v1:
time: 537 us; the launch traced here: 535 us
  waiting for transfers between devices  216 us (40%)
  other arithmetic  128 us (24%)
  matrix products  121 us (23%)
  local copies, waits for them, and re-layouts  32.3 us (6%)
  starting transfers between devices  23.2 us (4%)
  between operations  14.2 us (3%)
    ppermute x10, waiting for transfers between devices, from_partner(): lax.ppermute(array, axis, [(i, i ^ 1 << distance) for i in range(lax.axis...  168 us
    dot_general x16, matrix products, head_terms(): query_grad = jnp.dot(coef, stud_key, preferred_element_type=jnp.float32)  37.8 us
    dot_general x16, matrix products, head_terms(): jnp.dot(teach_query, teach_key.T, preferred_element_type=jnp.float32)  34.1 us
    convert_element_type x16, other arithmetic, head_terms(): (256.0 * stud_dim ** (-0.5) * (stud_prob - teach_prob)).astype(jnp.bfloat16)  31.4 us
    select_n x8, other arithmetic, shards(): jnp.where(upper_half, jnp.concatenate([theirs, mine], 0), jnp.concatenate...  28.7 us
    reduce_sum x16, other arithmetic, head_terms(): stud_prob = jax.nn.softmax(stud_scores, axis=-1)  28.5 us
    dot_general x16, matrix products, head_terms(): jnp.dot(stud_query, stud_key.T, preferred_element_type=jnp.float32)  28.2 us
    ppermute x2, waiting for transfers between devices, collect(): from_left = lax.ppermute(from_left, axis, ahead)  23.2 us
  transfers between devices with their start and end apart: 14, of which 9 were waited for; matrix products, arithmetic and copies ran while one was open for 28% of the time, Pallas kernels for 0%

profile of v1, /device:TPU:0, one launch (start us, length us, event | category | flops | bytes accessed | tf_op | source)
XLA Modules:
  0.0 535.1 jit_solution(8413722543100575426)
XLA Ops:
  7.2 4.0 copy.11
  11.7 4.1 collective-permute-done.2
  15.9 6.6 %maximum_select_fusion.2 = bf16[1024,2048]{0,1:T(8,128)(2,1)} fusion(bf16[512,2048]{0,1:T(8,128)(2,1)} %copy.11, bf16[512,2048]{0,1:T(8,128)(2,1)} %collective-permute-done.2, pred[]{:T(512)S(6)} %eq.18), kind=kLoop, calls=%fused_computation.66 | loop fusion | flops 18874368 | bytes 8388609 | tf_op jit(solution)/shard_map/jit(_where)/select_n | solution.py:88
  22.5 2.9 collective-permute-start.3
  25.7 3.9 copy.20
  33.3 2.6 maximum_select_fusion.8
  43.0 96.5 %collective-permute-done.1 = bf16[1024,512]{0,1:T(8,128)(2,1)} collective-permute-done((bf16[1024,512]{0,1:T(8,128)(2,1)}, bf16[1024,512]{0,1:T(8,128)(2,1)}, u32[]{:S(2)}, u32[]{:S(2)}) %collective-permute-start.1) | collective-permute-done | bytes 1048608 | tf_op jit(solution)/shard_map/ppermute | solution.py:32
  139.5 3.7 fusion.47
  143.2 18.3 %collective-permute-done.5 = bf16[1024,512]{0,1:T(8,128)(2,1)} collective-permute-done((bf16[1024,512]{0,1:T(8,128)(2,1)}, bf16[1024,512]{0,1:T(8,128)(2,1)}, u32[]{:S(2)}, u32[]{:S(2)}) %collective-permute-start.5) | collective-permute-done | bytes 1048608 | tf_op jit(solution)/shard_map/ppermute | solution.py:32
  161.5 3.7 fusion.48
  165.1 4.9 maximum_select_fusion.4
  171.8 5.3 maximum_select_fusion.3
  177.1 5.0 maximum_select_fusion.5
  182.1 8.9 %fusion.44 = bf16[8,2048,256]{1,2,0:T(8,128)(2,1)} fusion(bf16[1024,8,256]{0,2,1:T(8,128)(2,1)S(1)} %maximum_select_fusion.3, bf16[1024,8,256]{0,2,1:T(8,128)(2,1)} %bitcast.19, pred[]{:T(512)S(6)} %eq.17), kind=kLoop, calls=%fused_computation.59 | loop fusion | flops 37748736 | bytes 16777216 | tf_op jit(solution)/shard_map/transpose | solution.py:53
  191.0 2.5 broadcast.51.clone.1
  194.7 90.5 %while.24 = (s32[]{:T(128)}, f32[8,512,64]{1,2,0:T(8,128)}, f32[8,2048,64]{1,2,0:T(8,128)}, bf16[8,512,64]{1,2,0:T(8,128)(2,1)S(1)}, bf16[8,2048,64]{1,2,0:T(8,1...) while((s32[]{:T(128)}, f32[8,512,64]{1,2,0:T(8,128)}, ...), condition=%wide.region_5.6_spmd, body=%wide.region_0.5_spmd.sunk | while | flops 959444992 | bytes 34103380 | solution.py:60
  203.6 2.4 fusion.74
  214.9 2.4 fusion.74
  226.3 2.4 fusion.74
  237.6 2.4 fusion.74
  241.7 2.1 multiply_reduce_fusion.9
  248.9 2.4 fusion.74
  260.2 2.4 fusion.74
  271.5 2.4 fusion.74
  282.8 2.4 fusion.74
  285.2 11.2 %fusion.45 = bf16[8,2048,256]{1,2,0:T(8,128)(2,1)} fusion(bf16[1024,8,256]{0,2,1:T(8,128)(2,1)} %maximum_select_fusion.5, bf16[1024,8,256]{0,2,1:T(8,128)(2,1)} %bitcast.33, pred[]{:T(512)S(6)} %eq.17), kind=kLoop, calls=%fused_computation.61 | loop fusion | flops 37748736 | bytes 16777216 | tf_op jit(solution)/shard_map/transpose | solution.py:53
  296.4 2.5 broadcast.51.clone
  300.0 90.5 %while.25 = (s32[]{:T(128)}, f32[8,512,64]{1,2,0:T(8,128)}, f32[8,2048,64]{1,2,0:T(8,128)}, bf16[8,512,64]{1,2,0:T(8,128)(2,1)S(1)}, bf16[8,2048,64]{1,2,0:T(8,1...) while((s32[]{:T(128)}, f32[8,512,64]{1,2,0:T(8,128)}, ...), condition=%wide.region_11.12_spmd, body=%wide.region_6.11_spmd.sunk | while | flops 959444992 | bytes 34103380 | solution.py:60
  309.0 2.4 fusion.81
  320.3 2.4 fusion.81
  331.6 2.4 fusion.81
  342.9 2.4 fusion.81
  354.2 2.4 fusion.81
  365.5 2.4 fusion.81
  376.8 2.4 fusion.81
  388.1 2.4 fusion.81
  390.5 4.1 select_convert_fusion
  394.9 46.3 %collective-permute-done.8 = bf16[1024,1024]{0,1:T(8,128)(2,1)S(1)} collective-permute-done((bf16[1024,1024]{0,1:T(8,128)(2,1)S(1)}, bf16[1024,1024]{0,1:T(8,128)(2,1)S(1)}, u32[]{:S(2)}, u32[]{:S(2)}) %collective-permute-start.8) | collective-permute-done | bytes 2097184 | tf_op jit(solution)/shard_map/ppermute | solution.py:32
  441.2 4.5 convert_add_fusion
  445.9 2.6 collective-permute-done.9
  449.2 2.7 fusion.49
  453.6 2.2 collective-permute-start.11
  455.8 16.7 %collective-permute-done.10 = bf16[512,512]{0,1:T(8,128)(2,1)} collective-permute-done((bf16[512,512]{0,1:T(8,128)(2,1)S(1)}, bf16[512,512]{0,1:T(8,128)(2,1)}, u32[]{:S(2)}, u32[]{:S(2)}) %collective-permute-start.10) | collective-permute-done | bytes 524320 | tf_op jit(solution)/shard_map/ppermute | solution.py:19
  472.5 11.1 %collective-permute-start.12 = (bf16[512,512]{0,1:T(8,128)(2,1)}, bf16[512,512]{0,1:T(8,128)(2,1)}, u32[]{:S(2)}, u32[]{:S(2)}) collective-permute-start(bf16[512,512]{0,1:T(8,128)(2,1)} %collective-permute-done.10), channel_id=1, source_target_pairs={{0,8},{8,16},{16,24},{24,0},{1,9},{9,17},{17,25},{25,1},{2,10},{10... | collective-permute-start | bytes 1572872 | tf_op jit(solution)/shard_map/ppermute | solution.py:19
  487.5 19.6 %collective-permute-done.11 = bf16[512,512]{0,1:T(8,128)(2,1)} collective-permute-done((bf16[512,512]{0,1:T(8,128)(2,1)S(1)}, bf16[512,512]{0,1:T(8,128)(2,1)}, u32[]{:S(2)}, u32[]{:S(2)}) %collective-permute-start.11) | collective-permute-done | bytes 524320 | tf_op jit(solution)/shard_map/ppermute | solution.py:24
  510.2 6.5 %collective-permute-done.12 = bf16[512,512]{0,1:T(8,128)(2,1)} collective-permute-done((bf16[512,512]{0,1:T(8,128)(2,1)}, bf16[512,512]{0,1:T(8,128)(2,1)}, u32[]{:S(2)}, u32[]{:S(2)}) %collective-permute-start.12) | collective-permute-done | bytes 524320 | tf_op jit(solution)/shard_map/ppermute | solution.py:19
  518.8 5.6 %all-gather.2.cloned.1.call-done = bf16[512,2048]{0,1:T(8,128)(2,1)} async-done(((bf16[512,512]{0,1:T(8,128)(2,1)}), bf16[512,2048]{0,1:T(8,128)(2,1)}) %all-gather.2.cloned.1.call-update) | async-done | bytes 2097168 | tf_op jit(solution)/shard_map/all_gather | solution.py:111
  524.4 3.9 copy.32
  (122 shorter events, 168.4 us)
Async XLA Ops:
  7.2 18.2 %copy-start = (bf16[512,2048]{1,0:T(8,128)(2,1)S(1)}, bf16[512,2048]{1,0:T(8,128)(2,1)}, u32[]{:S(2)}) copy-start(bf16[512,2048]{1,0:T(8,128)(2,1)} %param.10) | copy-start | bytes 6291460
  7.2 517.2 %all-gather.2.cloned.1.call-start = ((), (), s32[]{:S(2)}) async-start(), calls=%async_computation | async-start | bytes 2621440 | tf_op jit(solution)/shard_map/all_gather | solution.py:111
  11.3 4.6 collective-permute-start.2
  22.5 159.6 %collective-permute-start.3 = (bf16[1024,2048]{0,1:T(8,128)(2,1)}, bf16[1024,2048]{0,1:T(8,128)(2,1)}, u32[]{:S(2)}, u32[]{:S(2)}) collective-permute-start(bf16[1024,2048]{0,1:T(8,128)(2,1)} %maximum_select_fusion.2), channel_id=1, source_target_pairs={{0,2},{1,3},{2,0},{3,1},{4,6},{5,7},{6,4},{7,5},{8,10},{9,11},{10,... | collective-permute-start | bytes 12582920 | tf_op jit(solution)/shard_map/ppermute | solution.py:32
  25.6 7.7 %collective-permute-start = (bf16[512,512]{0,1:T(8,128)(2,1)S(1)}, bf16[512,512]{0,1:T(8,128)(2,1)}, u32[]{:S(2)}, u32[]{:S(2)}) collective-permute-start(bf16[512,512]{0,1:T(8,128)(2,1)S(1)} %copy.41), channel_id=1, source_target_pairs={{0,1},{1,0},{2,3},{3,2},{4,5},{5,4},{6,7},{7,6},{8,9},{9,8},{10,11... | collective-permute-start | bytes 1572872 | tf_op jit(solution)/shard_map/ppermute | solution.py:32
  29.6 135.5 %collective-permute-start.6 = (bf16[512,2048]{0,1:T(8,128)(2,1)}, bf16[512,2048]{0,1:T(8,128)(2,1)S(1)}, u32[]{:S(2)}, u32[]{:S(2)}) collective-permute-start(bf16[512,2048]{0,1:T(8,128)(2,1)} %copy.20), channel_id=1, source_target_pairs={{0,1},{1,0},{2,3},{3,2},{4,5},{5,4},{6,7},{7,6},{8,9},{9,8},{10,11... | collective-permute-start | bytes 6291464 | tf_op jit(solution)/shard_map/ppermute | solution.py:32
  33.2 2.8 collective-permute-start.4
  35.9 103.6 %collective-permute-start.1 = (bf16[1024,512]{0,1:T(8,128)(2,1)}, bf16[1024,512]{0,1:T(8,128)(2,1)}, u32[]{:S(2)}, u32[]{:S(2)}) collective-permute-start(bf16[1024,512]{0,1:T(8,128)(2,1)} %maximum_select_fusion.8), channel_id=1, source_target_pairs={{0,2},{1,3},{2,0},{3,1},{4,6},{5,7},{6,4},{7,5},{8,10},{9,11},{10,... | collective-permute-start | bytes 3145736 | tf_op jit(solution)/shard_map/ppermute | solution.py:32
  36.0 0.8 copy-start.2
  38.1 123.4 %collective-permute-start.5 = (bf16[1024,512]{0,1:T(8,128)(2,1)}, bf16[1024,512]{0,1:T(8,128)(2,1)}, u32[]{:S(2)}, u32[]{:S(2)}) collective-permute-start(bf16[1024,512]{0,1:T(8,128)(2,1)} %maximum_select_fusion.10), channel_id=1, source_target_pairs={{0,2},{1,3},{2,0},{3,1},{4,6},{5,7},{6,4},{7,5},{8,10},{9,11},{10,... | collective-permute-start | bytes 3145736 | tf_op jit(solution)/shard_map/ppermute | solution.py:32
  170.1 115.1 %collective-permute-start.7 = (bf16[1024,2048]{0,1:T(8,128)(2,1)}, bf16[1024,2048]{0,1:T(8,128)(2,1)}, u32[]{:S(2)}, u32[]{:S(2)}) collective-permute-start(bf16[1024,2048]{0,1:T(8,128)(2,1)} %maximum_select_fusion.4), channel_id=1, source_target_pairs={{0,2},{1,3},{2,0},{3,1},{4,6},{5,7},{6,4},{7,5},{8,10},{9,11},{10,... | collective-permute-start | bytes 12582920 | tf_op jit(solution)/shard_map/ppermute | solution.py:32
  394.6 46.6 %collective-permute-start.8 = (bf16[1024,1024]{0,1:T(8,128)(2,1)S(1)}, bf16[1024,1024]{0,1:T(8,128)(2,1)S(1)}, u32[]{:S(2)}, u32[]{:S(2)}) collective-permute-start(bf16[1024,1024]{0,1:T(8,128)(2,1)S(1)} %select_convert_fusion), channel_id=1, source_target_pairs={{0,2},{1,3},{2,0},{3,1},{4,6},{5,7},{6,4},{7,5},{8,10},{9,11},{10,... | collective-permute-start | bytes 6291464 | tf_op jit(solution)/shard_map/ppermute | solution.py:32
  445.9 2.7 collective-permute-start.9
  452.0 20.6 %collective-permute-start.10 = (bf16[512,512]{0,1:T(8,128)(2,1)S(1)}, bf16[512,512]{0,1:T(8,128)(2,1)}, u32[]{:S(2)}, u32[]{:S(2)}) collective-permute-start(bf16[512,512]{0,1:T(8,128)(2,1)S(1)} %get-tuple-element.138), channel_id=1, source_target_pairs={{0,8},{8,16},{16,24},{24,0},{1,9},{9,17},{17,25},{25,1},{2,10},{10... | collective-permute-start | bytes 1572872 | tf_op jit(solution)/shard_map/ppermute | solution.py:19
  453.6 53.6 %collective-permute-start.11 = (bf16[512,512]{0,1:T(8,128)(2,1)S(1)}, bf16[512,512]{0,1:T(8,128)(2,1)}, u32[]{:S(2)}, u32[]{:S(2)}) collective-permute-start(bf16[512,512]{0,1:T(8,128)(2,1)S(1)} %get-tuple-element.138), channel_id=1, source_target_pairs={{0,24},{8,0},{16,8},{24,16},{1,25},{9,1},{17,9},{25,17},{2,26},{10... | collective-permute-start | bytes 1572872 | tf_op jit(solution)/shard_map/ppermute | solution.py:24
  472.5 44.2 %collective-permute-start.12 = (bf16[512,512]{0,1:T(8,128)(2,1)}, bf16[512,512]{0,1:T(8,128)(2,1)}, u32[]{:S(2)}, u32[]{:S(2)}) collective-permute-start(bf16[512,512]{0,1:T(8,128)(2,1)} %collective-permute-done.10), channel_id=1, source_target_pairs={{0,8},{8,16},{16,24},{24,0},{1,9},{9,17},{17,25},{25,1},{2,10},{10... | collective-permute-start | bytes 1572872 | tf_op jit(solution)/shard_map/ppermute | solution.py:19
  507.1 21.2 %copy-start.1 = (bf16[512,2048]{1,0:T(8,128)(2,1)S(1)}, bf16[512,2048]{1,0:T(8,128)(2,1)}, u32[]{:S(2)}) copy-start(bf16[512,2048]{1,0:T(8,128)(2,1)} %param.10) | copy-start | bytes 6291460
Sparse Core Ops, SparseCore 0:
  452.1 72.2 all-gather.1
